TPU v7x, 32 devices: a whole 2x2x4 slice. The times are simulated.
32 devices in a mesh: dp: 8 (over z, x), mp: 4 (over y, core).
Axes of the slice: x: 2, y: 2, z: 4, core: 2. Of those that a mesh axis runs over, the one named last changes fastest.
Arguments:
- tokens: bfloat16 [18944, 768], P(('dp', 'mp')), may hold values from -6 to 6
- image_group: int32 [8], P('dp'), may hold values from 0 to 1, as said below
- positions: int32 [2, 18944], P(None, 'dp'), may hold values from 0 to 23, as said below
- keep_mask: int32 [18944], P('dp'), may hold values from 0 to 1, as said below
- norm1_gain: float32 [768], replicated, may hold values from 0.25 to 1.75
- norm1_bias: float32 [768], replicated, may hold values from -1.75 to 1.75
- w_qkv: bfloat16 [768, 3, 768], P(None, None, 'mp'), may hold values from -0.21875 to 0.21875
- b_qkv: float32 [3, 768], P(None, 'mp'), may hold values from -1.75 to 1.75
- rotary_freqs: float32 [2, 12, 32], P(None, 'mp'), may hold values from -1 to 1
- w_out: bfloat16 [768, 768], P('mp'), may hold values from -0.875 to 0.875
- b_out: float32 [768], replicated, may hold values from -1.75 to 1.75
- norm2_gain: float32 [768], replicated, may hold values from 0.25 to 1.75
- norm2_bias: float32 [768], replicated, may hold values from -1.75 to 1.75
- w_up: bfloat16 [768, 3072], P(None, 'mp'), may hold values from -0.21875 to 0.21875
- b_up: bfloat16 [3072], P('mp'), may hold values from -1.75 to 1.75
- w_down: bfloat16 [3072, 768], P('mp'), may hold values from -0.109375 to 0.109375
- b_down: float32 [768], replicated, may hold values from -1.75 to 1.75
- cotangent: float32 [18944, 768], P(('dp', 'mp')), may hold values from -6 to 6
Outputs:
- output: bfloat16 [18944, 768], P(('dp', 'mp'))
- grad_tokens: float32 [18944, 768], P(('dp', 'mp'))
- grad_norm1_gain: float32 [768], replicated
- grad_norm1_bias: float32 [768], replicated
- grad_w_qkv: float32 [768, 3, 768], P(None, None, 'mp')
- grad_b_qkv: float32 [3, 768], P(None, 'mp')
- grad_rotary_freqs: float32 [2, 12, 32], P(None, 'mp')
- grad_w_out: float32 [768, 768], P('mp')
- grad_b_out: float32 [768], replicated
- grad_norm2_gain: float32 [768], replicated
- grad_norm2_bias: float32 [768], replicated
- grad_w_up: float32 [768, 3072], P(None, 'mp')
- grad_b_up: float32 [3072], P('mp')
- grad_w_down: float32 [3072, 768], P('mp')
- grad_b_down: float32 [768], replicated
Inputs may be any that keep to these rules, and one draw needn't show every extreme that they name: `image_group`: exactly 4 entries are 1. `positions`: each image's slots carry each of its patches once; padding slots carry 0, 0. `keep_mask`: in each image the kept slots are its first ones, at least one; padding slots are 0.
All inputs are finite; a program needn't handle non-finite values.
Results may differ from a plain program's by a relative error of at most 0.012.
The roundings to bfloat16 on the way count: a program that leaves them out, or rounds other values in their place, can miss the bound.
Values may be sent and summed in bfloat16 or wider, within the bound.
A program may use at most 192 MiB of HBM per device.

v0:
```python
import math
import functools

import jax
import jax.numpy as jnp
from jax import lax
from jax.experimental import pallas as pl
from jax.experimental.pallas import tpu as pltpu
from jax.sharding import PartitionSpec as P

HD = 64
SIDE_SMALL = 14
SIDE_LARGE = 24
IMG_SMALL = 3
IMG_LARGE = 1
NORM_EPS = 1e-06
HIDE = -1e30
BF = jnp.bfloat16
F32 = jnp.float32
SCALE = 1.0 / math.sqrt(HD)
HALF = HD // 2
LANES = 128
AUG = HD + 16


def nn(a, b):
    return jnp.dot(a, b, preferred_element_type=F32)


def tn(a, b):
    return lax.dot_general(a, b, (((0,), (0,)), ((), ())), preferred_element_type=F32)


def nt(a, b):
    return lax.dot_general(a, b, (((1,), (1,)), ((), ())), preferred_element_type=F32)


def unit_of(values):
    mean = jnp.mean(values, axis=-1, keepdims=True)
    centered = values - mean
    variance = jnp.mean(centered * centered, axis=-1, keepdims=True)
    scale = lax.rsqrt(variance + NORM_EPS)
    return centered * scale, scale


def norm_back(grad, unit, scale, gain):
    u = grad * gain
    mean_u = jnp.mean(u, axis=-1, keepdims=True)
    mean_un = jnp.mean(u * unit, axis=-1, keepdims=True)
    return scale * (u - mean_u - unit * mean_un)


def gelu_both(v):
    cdf = 0.5 * (1.0 + lax.erf(v * (1.0 / math.sqrt(2.0))))
    pdf = jnp.exp(-0.5 * v * v) * (1.0 / math.sqrt(2.0 * math.pi))
    return v * cdf, cdf + v * pdf


def pad_rows(value, rows):
    return jnp.concatenate(
        [value, jnp.zeros((rows - value.shape[0],) + value.shape[1:], value.dtype)]
    )


def first_norm(tokens, vec, normed1):
    unit, _ = unit_of(tokens[...].astype(F32))
    normed = (unit * vec[0:1] + vec[1:2]).astype(BF)
    normed1[...] = pad_rows(normed, normed1.shape[0])


def masks(rows, place, group, feats, keep):
    wide = place.shape[1]
    slot = lax.broadcasted_iota(jnp.int32, (16, wide), 1)
    row = lax.broadcasted_iota(jnp.int32, (16, wide), 0)
    image_id = jnp.zeros((16, wide), jnp.int32)
    for is_large, side, images in ((0, SIDE_SMALL, IMG_SMALL), (1, SIDE_LARGE, IMG_LARGE)):
        mine = sum([(slot >= n * side * side).astype(jnp.int32) for n in range(1, images)], jnp.zeros((16, wide), jnp.int32))
        image_id = jnp.where(group[0] == is_large, mine, image_id)
    same = (image_id == row) & (row < max(IMG_SMALL, IMG_LARGE))
    hidden = jnp.logical_not(same & (place[2:3] > 0.5)) & (row < max(IMG_SMALL, IMG_LARGE))
    feats[0] = jnp.where(same, 1.0, 0.0).astype(BF)
    feats[1] = jnp.where(hidden, HIDE, 0.0).astype(BF)
    feats[2] = jnp.where(row == 0, 1.0, 0.0).astype(BF)
    keep[...] = place[...].T[:rows, 2:3]


def attend_chunk(r, heads, rows, normed1, weights, hook, small, place, feats, q_all, k_all, v_all, lse, att, cosine, sine, proj):
    local = heads * HD
    column = small[r].T[:, 1:2]
    f0 = column[3 * local : 3 * local + heads * HALF]
    f1 = column[3 * local + heads * HALF : 3 * local + 2 * heads * HALF]
    angles = f0 * place[0:1] + f1 * place[1:2]
    cosine[r] = jnp.cos(angles)
    sine[r] = jnp.sin(angles)
    proj[...] = nt(weights[r, : 3 * local], normed1[...]) + column[: 3 * local]
    hook()
    for h in range(heads):
        cos_h = cosine[r, h * HALF : (h + 1) * HALF]
        sin_h = sine[r, h * HALF : (h + 1) * HALF]
        at = r * heads + h
        for base, ref, scale in ((0, q_all, SCALE), (local, k_all, 1.0)):
            a = proj[base + h * HD : base + h * HD + HALF]
            b = proj[base + h * HD + HALF : base + (h + 1) * HD]
            ref[at, :HALF] = ((a * cos_h - b * sin_h) * scale).astype(BF)
            ref[at, HALF:HD] = ((b * cos_h + a * sin_h) * scale).astype(BF)
        v_all[at, :HD] = proj[2 * local + h * HD : 2 * local + (h + 1) * HD].astype(BF)
        q_all[at, HD:] = feats[0]
        k_all[at, HD:] = feats[1]
        v_all[at, HD:] = feats[2]

    def head(h, carry):
        at = r * heads + h
        scores = tn(k_all[at, :, :rows], q_all[at])
        top = jnp.max(scores, axis=0, keepdims=True)
        terms = jnp.exp(scores - top).astype(BF)
        mixed = nn(v_all[at, :, :rows], terms)
        total = mixed[HD : HD + 1]
        att[pl.ds(pl.multiple_of(at * HD, HD), HD)] = (mixed[:HD] * (1.0 / total)).astype(BF)
        lse[at] = jnp.broadcast_to(top + jnp.log(total), lse.shape[1:])
        return carry

    lax.fori_loop(0, heads, head, 0)


def second_norm(rows, tokens, vec, att, wo, middle, normed2):
    branch = tn(att[...], wo)
    middle[...] = tokens[...].astype(F32) + branch[:rows] + vec[4:5]
    unit, _ = unit_of(middle[...])
    normed2[...] = (unit * vec[2:3] + vec[3:4]).astype(BF)


def mlp_chunk(r, normed2, g, wu, wd, small, mlp, gsecond, target, sums, active, slope, hook):
    width = normed2.shape[1]
    hidden = nn(normed2[...], wu[...]) + small[r][0:1]
    act, der = gelu_both(hidden)
    active[...] = act.astype(BF)
    slope[...] = der
    hook(0)
    target[width:] = tn(active[...], g[...]).astype(BF)
    mlp[...] += nn(active[...], wd[...])
    hook(1)
    gh = nt(g[...], wd[...]) * slope[...]
    active[...] = gh.astype(BF)
    sums[r] = jnp.sum(active[...].astype(F32), axis=0, keepdims=True)
    hook(2)
    target[:width] = tn(normed2[...], active[...]).astype(BF)
    gsecond[...] += nt(active[...], wu[...])


def finish_mlp(cot, keep, vec, middle, mlp, gsecond, g, out, branch, sums_vec):
    out[...] = (middle[...] + mlp[...] + vec[5:6]).astype(BF)
    unit, scale = unit_of(middle[...])
    grad = gsecond[...]
    gm = cot[...] * keep[...] + norm_back(grad, unit, scale, vec[2:3])
    low = gm.astype(BF)
    sums_vec[...] = jnp.concatenate(
        [
            jnp.sum(low.astype(F32), axis=0, keepdims=True),
            jnp.sum(grad * unit, axis=0, keepdims=True),
            jnp.sum(grad, axis=0, keepdims=True),
            jnp.sum(g[...].astype(F32), axis=0, keepdims=True),
            jnp.full((4, grad.shape[1]), 1.0, F32) * jnp.sum(keep[...]),
        ]
    )
    middle[...] = gm
    branch[...] = pad_rows(low, branch.shape[0])


def attend_back(at, heads, rows, q_all, k_all, v_all, lse, att, gatt, cosine, sine, place, gqkv, column, sums):
    local = heads * HD
    r, h = at // heads, at % heads
    here = pl.ds(pl.multiple_of(at * HD, HD), HD)
    wide = q_all.shape[2]
    scores = tn(k_all[at, :, :rows], q_all[at])
    probs = jnp.exp(scores - lse[at, 0:1])
    go = gatt[here]
    inner = jnp.sum(go.astype(F32) * att[here].astype(F32), axis=0, keepdims=True)
    gp = tn(v_all[at, :HD, :rows], go)
    gs = (probs * (gp - inner)).astype(BF)
    gv = nt(go, probs.astype(BF))
    gk = nt(q_all[at, :HD], gs)
    gq = nn(k_all[at, :HD, :rows], gs) * SCALE
    hs = pl.ds(pl.multiple_of(h * HALF, HALF), HALF)
    cos_h, sin_h = cosine[r, hs], sine[r, hs]
    term = jnp.zeros((HALF, wide), F32)
    pad = jnp.zeros((HD, wide - rows), F32)
    gk = jnp.concatenate([gk, pad], axis=1)
    gv = jnp.concatenate([gv, pad], axis=1)
    lows = []
    for ref, grad, back in ((q_all, gq, 1.0 / SCALE), (k_all, gk, 1.0)):
        a, b = grad[:HALF], grad[HALF:]
        ra = ref[at, :HALF].astype(F32)
        rb = ref[at, HALF:HD].astype(F32)
        term += (b * ra - a * rb) * back
        lows.append(jnp.concatenate([a * cos_h + b * sin_h, b * cos_h - a * sin_h], axis=0).astype(BF))
    lows.append(gv.astype(BF))
    for n, low in enumerate(lows):
        gqkv[r, pl.ds(pl.multiple_of(n * local + h * HD, HD), HD)] = low
        total = jnp.sum(low.astype(F32), axis=1, keepdims=True)
        column[n * HD : (n + 1) * HD] = jnp.broadcast_to(total, (HD, LANES))
    for n in range(2):
        total = jnp.sum(term * place[n : n + 1], axis=1, keepdims=True)
        column[3 * HD + n * HALF : 3 * HD + (n + 1) * HALF] = jnp.broadcast_to(total, (HALF, LANES))
    sums[pl.ds(at, 1)] = column[...].T[0:1]


UNIT = 128
PIECE = 192
LAGS = (1, 3, 5, 6)
PLAN = (1, 1, 3, 4, 9, 10, 11, 12, 13)
SLOTS = 6
TILE = 16
BITS_MP = (1, 2)


def flip(axis, bit):
    me = lax.axis_index(axis)
    return {axis: me + bit * (1 - 2 * ((me // bit) % 2))}


def bit_of(axis, bit):
    return (lax.axis_index(axis) // bit) % 2


def powers(axis):
    size = lax.axis_size(axis)
    return [1 << k for k in range(size.bit_length() - 1)]


def greet(peers):
    barrier = pltpu.get_barrier_semaphore()
    for peer in peers:
        pl.semaphore_signal(barrier, inc=1, device_id=peer, device_id_type=pl.DeviceIdType.MESH)
    pl.semaphore_wait(barrier, len(peers))


def remote(src, dst, send, recv, peer):
    return pltpu.make_async_remote_copy(
        src_ref=src, dst_ref=dst, send_sem=send, recv_sem=recv, device_id=peer, device_id_type=pl.DeviceIdType.MESH
    )


def steps_of(bits):
    return [UNIT // 2, UNIT // 8] + [UNIT // 8] * (len(bits) - 3)


def quad_peer(bits, step):
    one, two = bit_of("dp", bits[0]), bit_of("dp", bits[1])
    other_one = 1 - one if step & 1 else one
    other_two = 1 - two if step & 2 else two
    me = lax.axis_index("dp")
    return {"dp": me + bits[0] * (other_one - one) + bits[1] * (other_two - two)}, other_one + 2 * other_two


class Gather:
    def __init__(self, shards, full, cuts, send, recv, send_w, recv_w, local):
        self.shards, self.full = shards, full
        self.upper = bit_of("dp", 1)
        self.pieces = []
        for w, cut in enumerate(cuts):
            half = shards[w].shape[0] // 2
            for n in range(cut):
                self.pieces.append((w, half, n * (half // cut), half // cut))
        self.send, self.recv = send, recv
        self.send_w, self.recv_w, self.local = send_w, recv_w, local

    def rows(self, i, upper):
        _, half, start, size = self.pieces[i]
        return pl.ds(pl.multiple_of(upper * half + start, TILE), size)

    def pass_on(self, i, stage, source, target, rows, peer):
        w = self.pieces[i][0]
        full = self.full[w]
        src = self.shards[w].at[rows] if source is None else full.at[source, rows]
        return remote(src, full.at[target, rows], self.send.at[stage, i], self.recv.at[stage, i], peer)

    def across(self, i):
        return self.pass_on(i, 0, None, 2, self.rows(i, self.upper), flip("mp", 2))

    def beside(self, i):
        return self.pass_on(i, 1, 2, 2, self.rows(i, self.upper), flip("dp", 1))

    def near_half(self, i):
        return self.pass_on(i, 2, 2, 3, self.rows(i, self.upper), flip("mp", 1))

    def far_half(self, i):
        return self.pass_on(i, 3, 2, 3, self.rows(i, 1 - self.upper), flip("mp", 1))

    def whole(self, w):
        return remote(self.shards[w], self.full[w].at[1], self.send_w.at[w], self.recv_w.at[w], flip("mp", 1))

    def own(self, w):
        return pltpu.make_async_copy(self.shards[w], self.full[w].at[0], self.local.at[w])

    def got_across(self, i):
        self.across(i).wait()
        self.beside(i).start()
        self.near_half(i).start()
        if i + DEPTH < len(self.pieces):
            self.across(i + DEPTH).start()

    def got_beside(self, i):
        self.beside(i).wait()
        self.far_half(i).start()

    def got_all(self, i):
        self.near_half(i).wait()
        self.far_half(i).wait()


class Gather:
    def __init__(self, weights, send, recv):
        self.weights, self.send, self.recv = weights, send, recv
        self.pieces = weights.shape[1] // PIECE
        self.sub = PIECE // 4
        self.ticks = self.pieces + LAGS[-1]

    def place(self, u):
        one, two = bit_of("dp", 1), bit_of("dp", 2)
        first, second = flip("dp", 1)["dp"], flip("dp", 2)["dp"]
        odd = u % 2
        return (
            one + odd * (two - one),
            two + odd * (one - two),
            {"dp": first + odd * (second - first)},
            {"dp": second + odd * (first - second)},
        )

    def rows(self, u, quarter, count):
        return pl.ds(pl.multiple_of(u * PIECE + quarter * self.sub, TILE), count * self.sub)

    def copy(self, stage, u, source, target, rows, peer):
        return remote(
            self.weights.at[source, rows],
            self.weights.at[target, rows],
            self.send.at[stage, u],
            self.recv.at[stage, u],
            peer,
        )

    def own(self, u):
        return self.copy(0, u, 0, 1, self.rows(u, 0, 4), flip("mp", 1))

    def across(self, u):
        a, b, _, _ = self.place(u)
        return self.copy(1, u, 0, 2, self.rows(u, 2 * b + a, 1), flip("mp", 2))

    def quarter(self, u):
        a, b, peer, _ = self.place(u)
        return self.copy(2, u, 2, 2, self.rows(u, 2 * b + a, 1), peer)

    def half(self, u):
        _, b, _, peer = self.place(u)
        return self.copy(3, u, 2, 2, self.rows(u, 2 * b, 2), peer)

    def pass_on(self, u, n):
        a, b, _, _ = self.place(u)
        rows = (self.rows(u, 2 * b + a, 1), self.rows(u, 2 * b + 1 - a, 1), self.rows(u, 2 * (1 - b), 2))[n]
        return self.copy(4 + n, u, 2, 3, rows, flip("mp", 1))

    def owns(self, start, stop, begin):
        def each(u, carry):
            if begin:
                self.own(u).start()
            else:
                self.own(u).wait()
            return carry

        lax.fori_loop(start, stop, each, 0)

    def tick(self, t):
        def at(lag, body):
            u = t - lag

            @pl.when((u >= 0) & (u < self.pieces))
            def _():
                body(u)

        def begin(u):
            @pl.when(u == 0)
            def _():
                self.across(u).start()

            @pl.when(u + 1 < self.pieces)
            def _():
                self.across(u + 1).start()

        def got_across(u):
            self.across(u).wait()
            self.quarter(u).start()
            self.pass_on(u, 0).start()

        def got_quarter(u):
            self.quarter(u).wait()
            self.half(u).start()
            self.pass_on(u, 1).start()

        def got_half(u):
            self.half(u).wait()
            self.pass_on(u, 2).start()

        def got_all(u):
            for n in range(3):
                self.pass_on(u, n).wait()

        at(0, begin)
        for lag, body in zip(LAGS, (got_across, got_quarter, got_half, got_all)):
            at(lag, body)


class Reducer:
    def __init__(self, grads, got1, got3, got2, got_dp, send, recv):
        self.keep, self.near, self.cross, self.far = (grads.at[n] for n in range(4))
        self.total = self.near
        self.units = grads.shape[1] // UNIT
        self.got1, self.got3, self.got2 = got1, got3, got2
        self.got_half, self.got_quad, self.got_whole = got_dp[0], got_dp[1], got_dp[2:]
        self.send, self.recv = send, recv
        bits = powers("dp")
        self.bits, self.four, self.rest = bits[0], bits[1:3], bits[3:]
        self.half, self.quarter = UNIT // 2, UNIT // 8
        self.base = bit_of("dp", self.bits) * self.half
        self.offset = self.base + quad_peer(self.four, 0)[1] * self.quarter
        self.ticks = self.units + 7 + len(self.rest)

    def rows(self, u, size, offset=0):
        return pl.ds(pl.multiple_of(u * UNIT + offset, TILE), size)

    def slot(self, u, size):
        return pl.ds(pl.multiple_of((u % SLOTS) * size, TILE), size)

    def copy(self, stage, u, source, target, peer):
        return remote(source, target, self.send.at[stage, u], self.recv.at[stage, u], peer)

    def first(self, u):
        at, here, peer = self.rows(u, UNIT), self.slot(u, UNIT), flip("mp", 1)
        return (
            self.copy(0, u, self.near.at[at], self.got1.at[here], peer),
            self.copy(1, u, self.far.at[at], self.got3.at[here], peer),
        )

    def second(self, u):
        return self.copy(2, u, self.cross.at[self.rows(u, UNIT)], self.got2.at[self.slot(u, UNIT)], flip("mp", 2))

    def halve(self, u):
        source = self.keep.at[self.rows(u, self.half, self.half - self.base)]
        return self.copy(3, u, source, self.got_half.at[self.slot(u, self.half)], flip("dp", self.bits))

    def quads(self, u):
        copies = []
        for step in range(1, 4):
            peer, place = quad_peer(self.four, step)
            source = self.keep.at[self.rows(u, self.quarter, self.base + place * self.quarter)]
            target = self.got_quad.at[step - 1, self.slot(u, self.quarter)]
            copies.append(self.copy(3 + step, u, source, target, peer))
        return copies

    def whole(self, u, k):
        source = self.keep.at[self.rows(u, self.quarter, self.offset)]
        return self.copy(7 + k, u, source, self.got_whole[k].at[self.slot(u, self.quarter)], flip("dp", self.rest[k]))

    def quads_back(self, u):
        part = self.total.at[self.rows(u, self.quarter, self.offset)]
        first = 6 + len(self.rest)
        return [self.copy(first + step, u, part, part, quad_peer(self.four, step)[0]) for step in range(1, 4)]

    def half_back(self, u):
        part = self.total.at[self.rows(u, self.half, self.base)]
        return self.copy(10 + len(self.rest), u, part, part, flip("dp", self.bits))

    def add(self, source, target, u, size, offset, terms):
        def tile(i, carry):
            at = pl.ds(pl.multiple_of(u * UNIT + offset + i * TILE, TILE), TILE)
            value = source[at].astype(F32)
            for ref in terms:
                value += ref[pl.ds(pl.multiple_of((u % SLOTS) * size + i * TILE, TILE), TILE)].astype(F32)
            target[at] = value.astype(BF)
            return carry

        lax.fori_loop(0, size // TILE, tile, 0)

    def tick(self, t):
        rest = len(self.rest)

        def at(lag, body):
            u = t - lag

            @pl.when((u >= 0) & (u < self.units))
            def _():
                body(u)

        def each(copies, begin):
            for copy in copies:
                if begin:
                    copy.start()
                else:
                    copy.wait()

        def start_first(u):
            each(self.first(u), True)

        def after_first(u):
            each(self.first(u), False)
            self.add(self.cross, self.cross, u, UNIT, 0, [self.got3])
            self.second(u).start()

        def after_second(u):
            self.second(u).wait()
            self.add(self.keep, self.keep, u, UNIT, 0, [self.got1, self.got2])
            self.halve(u).start()

        def after_half(u):
            self.halve(u).wait()
            self.add(self.keep, self.keep, u, self.half, self.base, [self.got_half])
            each(self.quads(u), True)

        def after_quads(u):
            each(self.quads(u), False)
            terms = [self.got_quad.at[n] for n in range(3)]
            self.add(self.keep, self.keep if rest else self.total, u, self.quarter, self.offset, terms)
            each([self.whole(u, 0)] if rest else self.quads_back(u), True)

        def after_whole(k):
            def body(u):
                self.whole(u, k).wait()
                last = k == rest - 1
                target = self.total if last else self.keep
                self.add(self.keep, target, u, self.quarter, self.offset, [self.got_whole[k]])
                each(self.quads_back(u) if last else [self.whole(u, k + 1)], True)

            return body

        def after_quads_back(u):
            each(self.quads_back(u), False)
            self.half_back(u).start()

        def after_half_back(u):
            self.half_back(u).wait()

        at(0, start_first)
        at(1, after_first)
        at(3, after_second)
        at(4, after_half)
        at(5, after_quads)
        for k in range(rest):
            at(6 + k, after_whole(k))
        at(6 + rest, after_quads_back)
        at(7 + rest, after_half_back)


class SmallSum:
    def __init__(self, value, got, send, recv):
        self.value, self.got, self.send, self.recv = value, got, send, recv
        self.peers = [flip("mp", b) for b in BITS_MP] + [flip("dp", b) for b in powers("dp")]

    def copy(self, k):
        return remote(self.value, self.got.at[k], self.send.at[k], self.recv.at[k], self.peers[k])

    def finish(self, k):
        self.copy(k).wait()
        value, got = self.value, self.got
        value[:8] += got[k, :8]
        if k == 0:
            value[8:10] += got[k, 10:12]
            value[12:14] += got[k, 14:16]
        elif k == 1:
            value[8:10] += got[k, 12:14]
        else:
            value[8:10] += got[k, 8:10]


def layer_body(
    heads,
    rows,
    tokens_in,
    gain1_in,
    bias1_in,
    gain2_in,
    bias2_in,
    bias_out_in,
    bias_down_in,
    positions_in,
    keep_mask_in,
    bias_qkv_in,
    freqs_in,
    bias_up_in,
    group,
    cot,
    s_qkv,
    s_out,
    s_up,
    s_down,
    out,
    gx,
    o_up,
    o_down,
    o_out,
    o_qkv,
    small_sum,
    factor_out,
    tokens,
    gain1,
    bias1,
    gain2,
    bias2,
    bias_out,
    bias_down,
    positions,
    keep_mask,
    bias_qkv,
    freqs,
    bias_up,
    all_w,
    small,
    place,
    q_all,
    k_all,
    v_all,
    lse,
    att,
    cosine,
    sine,
    normed1,
    middle,
    branch,
    g,
    mlp,
    gsecond,
    active,
    slope,
    vec,
    keep_col,
    feats,
    sums_up,
    sums_vec,
    column,
    head_sums,
    grads,
    got1,
    got3,
    got2,
    got_small,
    send_g,
    recv_g,
    send_s,
    recv_s,
    local_sem,
    send,
    recv,
    send_v,
    recv_v,
    *got_dp,
):
    parts, count = all_w.shape[0], q_all.shape[0]
    local = heads * HD
    width = tokens.shape[1]
    wide = q_all.shape[2]
    top = 4 * local
    units = (all_w.shape[1] - top) // 2
    mlp_rows = 2 * width
    up_rows, down_rows = pl.ds(top, width), pl.ds(top + width, units)
    loads, start = [], 0
    for n, ref in enumerate((s_qkv, s_out, s_up, s_down)):
        loads.append(pltpu.make_async_copy(ref, all_w.at[0, pl.ds(start, ref.shape[0])], local_sem.at[n]))
        start += ref.shape[0]
    load_cot = pltpu.make_async_copy(cot, slope, local_sem.at[5])
    early = []
    for n, (source, target) in enumerate(
        (
            (bias_up_in, bias_up),
            (bias_qkv_in, bias_qkv),
            (freqs_in, freqs),
            (tokens_in, tokens),
            (gain1_in, gain1),
            (bias1_in, bias1),
            (gain2_in, gain2),
            (bias2_in, bias2),
            (bias_out_in, bias_out),
            (bias_down_in, bias_down),
            (positions_in, positions),
            (keep_mask_in, keep_mask),
        )
    ):
        early.append(pltpu.make_async_copy(source, target, local_sem.at[12 + n]))
    for load in early[:3] + loads + early[3:]:
        load.start()
    for load in early[:3]:
        load.wait()
    small[0] = jnp.zeros_like(small[0])
    small[0, 0:1] = bias_up[...].reshape(1, units).astype(F32)
    row = [bias_qkv[n : n + 1] for n in range(3)] + [freqs[h, n : n + 1] for n in range(2) for h in range(heads)]
    small[0, 1:2] = jnp.concatenate(row, axis=1)
    both = {"mp": lax.axis_index("mp") + 1 * (1 - 2 * bit_of("mp", 1)) + 2 * (1 - 2 * bit_of("mp", 2))}
    sums = SmallSum(small_sum, got_small, send_v, recv_v)
    greet(sums.peers + [both])
    peers = [flip("mp", 1), flip("mp", 2), both]
    smalls = [
        remote(small.at[0], small.at[r], send_s.at[r - 1], recv_s.at[r - 1], peers[r - 1]) for r in range(1, 4)
    ]
    for copy in smalls:
        copy.start()
    weights = Gather(all_w, send_g, recv_g)
    for load in loads + early[3:]:
        load.wait()
    weights.tick(0)
    weights.owns(0, weights.pieces, True)
    load_cot.start()
    for n, ref in enumerate((gain1, bias1, gain2, bias2, bias_out, bias_down)):
        vec[n : n + 1] = ref[...].reshape(1, width)
    first_norm(tokens, vec, normed1)
    own_part = lax.axis_index("mp")
    spot = jnp.concatenate([positions[...], keep_mask[...].reshape(1, keep_mask.shape[0])])
    mine = spot[:, :rows]
    for n in range(1, parts):
        mine = jnp.where(own_part == n, spot[:, n * rows : (n + 1) * rows], mine)
    place[...] = jnp.zeros_like(place)
    place[0:3, :rows] = mine.astype(F32)
    masks(rows, place, group, feats, keep_col)
    for copy in smalls:
        copy.wait()
    proj = mlp.at[: 3 * local, :wide]

    def gather_step(t, carry):
        weights.tick(t)
        return carry

    reached = [1]

    def gather_to(n):
        if PLAN[n] > reached[0]:
            lax.fori_loop(reached[0], PLAN[n], gather_step, 0)
            reached[0] = PLAN[n]

    first_rows = 3 * local // PIECE
    for r in range(parts):
        gather_to(2 * r)
        if r == 1:
            weights.owns(0, first_rows, False)
        attend_chunk(
            r, heads, rows, normed1, all_w, functools.partial(gather_to, 2 * r + 1), small, place, feats,
            q_all, k_all, v_all, lse, att, cosine, sine, proj,
        )
    weights.owns(first_rows, weights.pieces, False)
    load_cot.wait()
    g[...] = (slope[...] * keep_col[...]).astype(BF)
    gather_to(2 * parts)
    done = reached[0]
    wo = jnp.concatenate([all_w[r, 3 * local : top] for r in range(parts)])
    normed2 = branch.at[:rows]
    second_norm(rows, tokens, vec, att, wo, middle, normed2)
    mlp[...] = jnp.zeros_like(mlp)
    gsecond[...] = jnp.zeros_like(gsecond)

    def mlp_step(r, carry):
        mlp_chunk(
            r, normed2, g, all_w.at[r, up_rows], all_w.at[r, down_rows], small, mlp, gsecond,
            grads.at[r, pl.ds(0, mlp_rows)], sums_up, active, slope, lambda n: weights.tick(done + 3 * r + n),
        )
        return carry

    assert done + 6 >= weights.ticks
    lax.fori_loop(0, parts, mlp_step, 0)
    load_cot.start()
    net = Reducer(grads, got1, got3, got2, got_dp, send, recv)

    def step(t, carry):
        net.tick(t)
        return carry

    def ticks(start, stop):
        lax.fori_loop(start, stop, step, 0)

    ticks(0, 1)
    load_cot.wait()
    finish_mlp(slope, keep_col, vec, middle, mlp, gsecond, g, active, branch, sums_vec)
    store_out = pltpu.make_async_copy(active, out, local_sem.at[6])
    store_out.start()
    ticks(1, 2)
    gatt = all_w.at[0, down_rows, :wide]
    gqkv = all_w.at[:, pl.ds(top, 3 * local), :wide]
    wo = jnp.concatenate([all_w[r, 3 * local : top] for r in range(parts)])
    gatt[...] = nt(wo, branch[...]).astype(BF)

    def some_heads(i, carry):
        net.tick(2 + i)

        def head(n, c):
            attend_back(2 * i + n, heads, rows, q_all, k_all, v_all, lse, att, gatt, cosine, sine, place, gqkv, column, head_sums)
            return c

        return lax.fori_loop(0, 2, head, carry)

    lax.fori_loop(0, count // 2, some_heads, 0)
    base = 2 + count // 2
    gsecond[...] = jnp.zeros_like(gsecond)

    def late(r, carry):
        net.tick(base + r)
        here = att[pl.ds(pl.multiple_of(r * local, HD), local)]
        grads[r, mlp_rows : mlp_rows + local] = nn(here, branch[...]).astype(BF)
        grads[r, mlp_rows + local :] = nn(gqkv[r], normed1[...]).astype(BF)
        gsecond[...] += tn(gqkv[r], all_w[r, : 3 * local])[:rows]
        return carry

    lax.fori_loop(0, parts, late, 0)
    base = base + parts
    ticks(base, base + 1)
    grad = gsecond[...]
    unit, scale = unit_of(tokens[...].astype(F32))
    gsecond[...] = middle[...] + norm_back(grad, unit, scale, vec[0:1])
    store_gx = pltpu.make_async_copy(gsecond, gx, local_sem.at[7])
    store_gx.start()
    small_sum[...] = jnp.zeros_like(small_sum)
    small_sum[0:1] = jnp.sum(grad * unit, axis=0, keepdims=True)
    small_sum[1:2] = jnp.sum(grad, axis=0, keepdims=True)
    small_sum[2:7] = sums_vec[0:5]
    for r in range(parts):
        small_sum[8 + 2 * r : 9 + 2 * r] = sums_up[r]
        mine = [head_sums[r * heads + h : r * heads + h + 1] for h in range(heads)]
        pieces = [v[:, n * HD : (n + 1) * HD] for n in range(3) for v in mine]
        pieces += [v[:, 3 * HD + n * HALF : 3 * HD + (n + 1) * HALF] for n in range(2) for v in mine]
        small_sum[9 + 2 * r : 10 + 2 * r] = jnp.concatenate(pieces, axis=1)
    base = base + 1
    exchanges = len(sums.peers)

    def step_small(t, carry):
        net.tick(t)
        for k in range(exchanges + 1):
            @pl.when(t == base + k)
            def _():
                if k > 0:
                    sums.finish(k - 1)
                if k == exchanges:
                    factor = lax.axis_size("dp") / small_sum[6:7]
                    factor_out[0] = factor[0, 0]
                    small_sum[...] *= factor
                if k < exchanges:
                    sums.copy(k).start()
        return carry

    lax.fori_loop(base, base + exchanges + 1, step_small, 0)
    ticks(base + exchanges + 1, max(net.ticks, base + exchanges + 1))
    stores = []
    start = 0
    for n, ref in enumerate((o_up, o_down, o_out, o_qkv)):
        stores.append(pltpu.make_async_copy(grads.at[1, pl.ds(start, ref.shape[0])], ref, local_sem.at[8 + n]))
        stores[-1].start()
        start += ref.shape[0]
    for copy in stores + [store_out, store_gx]:
        copy.wait()


def finish_body(vectors, local, up, down, out, qkv, small, factor, middle, gx, *rest):
    results, (held, held_gx, copies) = rest[:-3], rest[-3:]
    loads = [pltpu.make_async_copy(middle, held, copies.at[0]), pltpu.make_async_copy(gx, held_gx, copies.at[1])]
    moves = [pltpu.make_async_copy(held, results[-2], copies.at[2]), pltpu.make_async_copy(held_gx, results[-1], copies.at[3])]

    @pl.when(pl.program_id(0) == 0)
    def _():
        for load in loads:
            load.start()
        for n, row in enumerate(vectors):
            results[4 + n][...] = small[row : row + 1].reshape(small.shape[1])
        b_qkv, freqs = results[4 + len(vectors)], results[5 + len(vectors)]
        for n in range(3):
            b_qkv[n : n + 1] = small[9:10, n * local : (n + 1) * local]
        for n in range(2):
            for h in range(freqs.shape[0]):
                start = 3 * local + (n * freqs.shape[0] + h) * HALF
                freqs[h, n : n + 1] = small[9:10, start : start + HALF]

    for source, target in zip((up, down, out, qkv), results):
        target[...] = source[...].astype(F32) * factor[0]

    @pl.when(pl.program_id(0) == 2)
    def _():
        for load in loads:
            load.wait()
        for move in moves:
            move.start()

    @pl.when(pl.program_id(0) == pl.num_programs(0) - 1)
    def _():
        for move in moves:
            move.wait()


def sds(shape, dtype):
    return jax.ShapeDtypeStruct(shape, dtype)


def body(
    tokens,
    image_group,
    positions,
    keep_mask,
    norm1_gain,
    norm1_bias,
    w_qkv,
    b_qkv,
    rotary_freqs,
    w_out,
    b_out,
    norm2_gain,
    norm2_bias,
    w_up,
    b_up,
    w_down,
    b_down,
    cotangent,
):
    rows, width = tokens.shape
    wide = -(-rows // LANES) * LANES
    parts = lax.axis_size("mp")
    mp_index = lax.axis_index("mp")
    heads = rotary_freqs.shape[1]
    local = heads * HD
    units = w_up.shape[1]
    w_qkv_t = w_qkv.reshape(width, 3 * local).T
    count = parts * heads
    bits = powers("dp")
    sizes = steps_of(bits)
    stages = 8 + len(bits)
    total_rows = 2 * width + 4 * local
    unit_count = total_rows // UNIT
    pieces = total_rows // PIECE
    swaps = 2 + len(bits)
    in_vmem = pl.BlockSpec(memory_space=pltpu.VMEM)
    in_smem = pl.BlockSpec(memory_space=pltpu.SMEM)
    anywhere = pl.BlockSpec(memory_space=pl.ANY)
    dma = pltpu.SemaphoreType.DMA
    vmem = pltpu.VMEM
    out, gx, o_up, o_down, o_out, o_qkv, small_sum, factor = pl.pallas_call(
        functools.partial(layer_body, heads, rows),
        out_shape=[
            sds((rows, width), BF),
            sds((rows, width), F32),
            sds((width, units), BF),
            sds((units, width), BF),
            sds((local, width), BF),
            sds((3 * local, width), BF),
            sds((16, width), F32),
            sds((1,), F32),
        ],
        in_specs=[anywhere] * 12 + [in_smem] + [anywhere] * 5,
        out_specs=[anywhere] * 6 + [in_vmem, in_smem],
        scratch_shapes=[
            vmem(tokens.shape, BF),
        ]
        + [vmem((width,), F32)] * 6
        + [
            vmem(positions.shape, jnp.int32),
            vmem(keep_mask.shape, jnp.int32),
            vmem(b_qkv.shape, F32),
            vmem((heads, 2, HALF), F32),
            vmem(b_up.shape, BF),
            vmem((parts, total_rows, width), BF),
            vmem((parts, 8, width), F32),
            vmem((8, wide), F32),
            vmem((count, AUG, wide), BF),
            vmem((count, AUG, wide), BF),
            vmem((count, AUG, wide), BF),
            vmem((count, 8, wide), F32),
            vmem((count * HD, wide), BF),
            vmem((parts, heads * HALF, wide), F32),
            vmem((parts, heads * HALF, wide), F32),
            vmem((wide, width), BF),
            vmem((rows, width), F32),
            vmem((wide, width), BF),
            vmem((rows, width), BF),
            vmem((rows, width), F32),
            vmem((rows, width), F32),
            vmem((rows, units), BF),
            vmem((rows, units), F32),
            vmem((8, width), F32),
            vmem((rows, 1), F32),
            vmem((3, 16, wide), BF),
            vmem((parts, 1, units), F32),
            vmem((8, width), F32),
            vmem((3 * HD + 2 * HALF, LANES), F32),
            vmem((-(-count // 8) * 8, 3 * HD + 2 * HALF), F32),
            vmem((parts, total_rows, width), BF),
            vmem((SLOTS * UNIT, width), BF),
            vmem((SLOTS * UNIT, width), BF),
            vmem((SLOTS * UNIT, width), BF),
            vmem((swaps, 16, width), F32),
            dma((7, pieces)),
            dma((7, pieces)),
            dma((3,)),
            dma((3,)),
            dma((24,)),
            dma((stages, unit_count)),
            dma((stages, unit_count)),
            dma((swaps,)),
            dma((swaps,)),
        ]
        + [vmem((SLOTS * UNIT // 2, width), BF), vmem((3, SLOTS * UNIT // 8, width), BF)]
        + [vmem((SLOTS * size, width), BF) for size in sizes[2:]],
        compiler_params=pltpu.CompilerParams(vmem_limit_bytes=61 << 20, collective_id=0, has_side_effects=True),
    )(tokens, norm1_gain, norm1_bias, norm2_gain, norm2_bias, b_out, b_down, positions, keep_mask, b_qkv,
      rotary_freqs.transpose(1, 0, 2), b_up, image_group, cotangent, w_qkv_t, w_out, w_up, w_down)
    steps = 6

    def piece(ref):
        return pl.BlockSpec((ref.shape[0] // steps, width), lambda i: (i, 0))

    sums = (o_up, o_down, o_out, o_qkv)
    vectors = [0, 1, 2, 3, 4, 5, 8]
    finished = pl.pallas_call(
        functools.partial(finish_body, vectors, local),
        grid=(steps,),
        out_shape=[sds(ref.shape, F32) for ref in sums]
        + [sds((width,), F32)] * len(vectors)
        + [sds((3, local), F32), sds((heads, 2, HALF), F32), sds(out.shape, BF), sds(gx.shape, F32)],
        in_specs=[piece(ref) for ref in sums] + [in_vmem, in_smem, anywhere, anywhere],
        out_specs=[piece(ref) for ref in sums] + [in_vmem] * (len(vectors) + 2) + [anywhere] * 2,
        scratch_shapes=[vmem(out.shape, BF), vmem(gx.shape, F32), dma((4,))],
        compiler_params=pltpu.CompilerParams(vmem_limit_bytes=60 << 20),
    )(*sums, small_sum, factor, out, gx)
    sum_w_up, sum_w_down, sum_w_out, sum_w_qkv, gain1, bias1, b_out_sum, gain2, bias2, b_down_sum, b_up_sum = finished[:11]
    b_qkv_sum, freqs_sum, out, gx = finished[11:]
    return (
        out,
        gx,
        gain1,
        bias1,
        sum_w_qkv.T.reshape(w_qkv.shape),
        b_qkv_sum,
        freqs_sum.transpose(1, 0, 2),
        sum_w_out,
        b_out_sum,
        gain2,
        bias2,
        sum_w_up,
        b_up_sum,
        sum_w_down,
        b_down_sum,
    )


def solution(mesh):
    placed = (
        P(("dp", "mp"), None),
        P("dp"),
        P(None, "dp"),
        P("dp"),
        P(),
        P(),
        P(None, None, "mp"),
        P(None, "mp"),
        P(None, "mp", None),
        P("mp", None),
        P(),
        P(),
        P(),
        P(None, "mp"),
        P("mp"),
        P("mp", None),
        P(),
        P(("dp", "mp"), None),
    )
    return jax.shard_map(
        body,
        mesh=mesh,
        in_specs=placed,
        out_specs=(
            P(("dp", "mp"), None),
            P(("dp", "mp"), None),
            P(),
            P(),
            P(None, None, "mp"),
            P(None, "mp"),
            P(None, "mp", None),
            P("mp", None),
            P(),
            P(),
            P(),
            P(None, "mp"),
            P("mp"),
            P("mp", None),
            P(),
        ),
        check_vma=False,
    )
```

profile of v0, /device:TPU:0, one launch (start us, length us, event | category | flops | bytes accessed | tf_op | source)
XLA Modules:
  0.0 189.2 jit_solution(14112017320214226470)
XLA Ops:
  1.3 178.6 %shard_map.289 = (bf16[592,768]{1,0:T(8,128)(2,1)}, f32[592,768]{1,0:T(8,128)}, bf16[768,768]{1,0:T(8,128)(2,1)}, bf16[768,768]{1,0:T(8,128)(2,1)}, bf16[192,768...) custom-call(bf16[592,768]{1,0:T(8,128)(2,1)} %tokens_in.1, f32[768]{0:T(1024)} %gain1_in.1, ...), custom_call_target="tpu_custom_call" | custom-call | tf_op jit(solution)/shard_map/pallas_call | solution.py:933
  179.9 9.2 %shard_map.290 = (f32[768,768]{1,0:T(8,128)}, f32[768,768]{1,0:T(8,128)}, f32[192,768]{1,0:T(8,128)}, f32[576,768]{1,0:T(8,128)}, f32[768]{0:T(1024)}, /*index=5...) custom-call(bf16[768,768]{1,0:T(8,128)(2,1)} %get-tuple-element.38.u, ...), custom_call_target="tpu_custom_call" | custom-call | tf_op jit(solution)/shard_map/pallas_call | solution.py:1009
where the time goes:
time: 189 us
  Pallas kernels  188 us (99%)
    pallas_call x1, Pallas kernels, body(): pl.pallas_call(functools.partial(layer_body, heads, rows), out_shape=[sds...  179 us
    pallas_call x1, Pallas kernels, body(): pl.pallas_call(functools.partial(finish_body, vectors, local), grid=(step...  9.21 us

commit v1 on v0

--- a/solution.py
+++ b/solution.py
@@ -93,7 +93,7 @@
     cosine[r] = jnp.cos(angles)
     sine[r] = jnp.sin(angles)
     proj[...] = nt(weights[r, : 3 * local], normed1[...]) + column[: 3 * local]
-    hook()
+    hook(1)
     for h in range(heads):
         cos_h = cosine[r, h * HALF : (h + 1) * HALF]
         sin_h = sine[r, h * HALF : (h + 1) * HALF]
@@ -117,6 +117,8 @@
         total = mixed[HD : HD + 1]
         att[pl.ds(pl.multiple_of(at * HD, HD), HD)] = (mixed[:HD] * (1.0 / total)).astype(BF)
         lse[at] = jnp.broadcast_to(top + jnp.log(total), lse.shape[1:])
+        for n in range(heads - 1):
+            pl.when(h == n)(functools.partial(hook, 2 + n))
         return carry
 
     lax.fori_loop(0, heads, head, 0)
@@ -131,19 +133,21 @@
 
 def mlp_chunk(r, normed2, g, wu, wd, small, mlp, gsecond, target, sums, active, slope, hook):
     width = normed2.shape[1]
+    hook(-1)
     hidden = nn(normed2[...], wu[...]) + small[r][0:1]
     act, der = gelu_both(hidden)
     active[...] = act.astype(BF)
     slope[...] = der
     hook(0)
-    target[width:] = tn(active[...], g[...]).astype(BF)
+    target[: active.shape[1]] = tn(active[...], g[...]).astype(BF)
+    hook(1)
     mlp[...] += nn(active[...], wd[...])
-    hook(1)
     gh = nt(g[...], wd[...]) * slope[...]
     active[...] = gh.astype(BF)
     sums[r] = jnp.sum(active[...].astype(F32), axis=0, keepdims=True)
     hook(2)
-    target[:width] = tn(normed2[...], active[...]).astype(BF)
+    target[active.shape[1] :] = tn(normed2[...], active[...]).astype(BF)
+    hook(3)
     gsecond[...] += nt(active[...], wu[...])
 
 
@@ -206,8 +210,31 @@
 
 UNIT = 128
 PIECE = 192
-LAGS = (1, 3, 5, 6)
-PLAN = (1, 1, 3, 4, 9, 10, 11, 12, 13)
+DEPTH = 3
+PLAN = {
+    ('p', 0, 2): (('a', 0),),
+    ('p', 1, 1): (('a', 1),),
+    ('p', 1, 3): (('a', 2), ('b', 0)),
+    ('p', 2, 0): (('d', 0), ('a', 3), ('b', 1), ('d', 1), ('a', 4), ('b', 2)),
+    ('p', 2, 1): (('d', 2),),
+    ('p', 2, 2): (('b', 3), ('a', 5)),
+    ('p', 2, 3): (('d', 3),),
+    ('p', 3, 1): (('b', 4), ('a', 6)),
+    ('p', 3, 2): (('d', 4),),
+    ('p', 3, 3): (('a', 7), ('b', 5)),
+    ('w', 0, 0): (('d', 5),),
+    ('f', 0, 0): (('a', 8), ('b', 6)),
+    ('f', 0, 1): (('d', 6), ('a', 9), ('b', 7)),
+    ('f', 0, 2): (('d', 7),),
+    ('f', 0, 3): (('a', 10),),
+    ('f', 0, 4): (('b', 8),),
+    ('f', 1, 0): (('d', 8), ('a', 11)),
+    ('f', 1, 1): (('b', 9),),
+    ('f', 1, 2): (('d', 9),),
+    ('f', 1, 3): (('b', 10),),
+    ('f', 1, 4): (('d', 10), ('b', 11)),
+    ('f', 2, 0): (('d', 11),),
+}
 SLOTS = 6
 TILE = 16
 BITS_MP = (1, 2)
@@ -253,81 +280,14 @@
 
 
 class Gather:
-    def __init__(self, shards, full, cuts, send, recv, send_w, recv_w, local):
-        self.shards, self.full = shards, full
-        self.upper = bit_of("dp", 1)
-        self.pieces = []
-        for w, cut in enumerate(cuts):
-            half = shards[w].shape[0] // 2
-            for n in range(cut):
-                self.pieces.append((w, half, n * (half // cut), half // cut))
-        self.send, self.recv = send, recv
-        self.send_w, self.recv_w, self.local = send_w, recv_w, local
-
-    def rows(self, i, upper):
-        _, half, start, size = self.pieces[i]
-        return pl.ds(pl.multiple_of(upper * half + start, TILE), size)
-
-    def pass_on(self, i, stage, source, target, rows, peer):
-        w = self.pieces[i][0]
-        full = self.full[w]
-        src = self.shards[w].at[rows] if source is None else full.at[source, rows]
-        return remote(src, full.at[target, rows], self.send.at[stage, i], self.recv.at[stage, i], peer)
-
-    def across(self, i):
-        return self.pass_on(i, 0, None, 2, self.rows(i, self.upper), flip("mp", 2))
-
-    def beside(self, i):
-        return self.pass_on(i, 1, 2, 2, self.rows(i, self.upper), flip("dp", 1))
-
-    def near_half(self, i):
-        return self.pass_on(i, 2, 2, 3, self.rows(i, self.upper), flip("mp", 1))
-
-    def far_half(self, i):
-        return self.pass_on(i, 3, 2, 3, self.rows(i, 1 - self.upper), flip("mp", 1))
-
-    def whole(self, w):
-        return remote(self.shards[w], self.full[w].at[1], self.send_w.at[w], self.recv_w.at[w], flip("mp", 1))
-
-    def own(self, w):
-        return pltpu.make_async_copy(self.shards[w], self.full[w].at[0], self.local.at[w])
-
-    def got_across(self, i):
-        self.across(i).wait()
-        self.beside(i).start()
-        self.near_half(i).start()
-        if i + DEPTH < len(self.pieces):
-            self.across(i + DEPTH).start()
-
-    def got_beside(self, i):
-        self.beside(i).wait()
-        self.far_half(i).start()
-
-    def got_all(self, i):
-        self.near_half(i).wait()
-        self.far_half(i).wait()
-
-
-class Gather:
     def __init__(self, weights, send, recv):
         self.weights, self.send, self.recv = weights, send, recv
         self.pieces = weights.shape[1] // PIECE
-        self.sub = PIECE // 4
-        self.ticks = self.pieces + LAGS[-1]
-
-    def place(self, u):
-        one, two = bit_of("dp", 1), bit_of("dp", 2)
-        first, second = flip("dp", 1)["dp"], flip("dp", 2)["dp"]
-        odd = u % 2
-        return (
-            one + odd * (two - one),
-            two + odd * (one - two),
-            {"dp": first + odd * (second - first)},
-            {"dp": second + odd * (first - second)},
-        )
-
-    def rows(self, u, quarter, count):
-        return pl.ds(pl.multiple_of(u * PIECE + quarter * self.sub, TILE), count * self.sub)
+
+    def rows(self, u, mine):
+        half = PIECE // 2
+        upper = bit_of("dp", 1 + u % 2)
+        return pl.ds(pl.multiple_of(u * PIECE + (upper if mine else 1 - upper) * half, TILE), half)
 
     def copy(self, stage, u, source, target, rows, peer):
         return remote(
@@ -339,24 +299,16 @@
         )
 
     def own(self, u):
-        return self.copy(0, u, 0, 1, self.rows(u, 0, 4), flip("mp", 1))
+        return self.copy(0, u, 0, 1, pl.ds(pl.multiple_of(u * PIECE, TILE), PIECE), flip("mp", 1))
 
     def across(self, u):
-        a, b, _, _ = self.place(u)
-        return self.copy(1, u, 0, 2, self.rows(u, 2 * b + a, 1), flip("mp", 2))
-
-    def quarter(self, u):
-        a, b, peer, _ = self.place(u)
-        return self.copy(2, u, 2, 2, self.rows(u, 2 * b + a, 1), peer)
-
-    def half(self, u):
-        _, b, _, peer = self.place(u)
-        return self.copy(3, u, 2, 2, self.rows(u, 2 * b, 2), peer)
+        return self.copy(1, u, 0, 2, self.rows(u, True), flip("mp", 2))
+
+    def beside(self, u):
+        return self.copy(2, u, 2, 2, self.rows(u, True), flip("dp", 1 + u % 2))
 
     def pass_on(self, u, n):
-        a, b, _, _ = self.place(u)
-        rows = (self.rows(u, 2 * b + a, 1), self.rows(u, 2 * b + 1 - a, 1), self.rows(u, 2 * (1 - b), 2))[n]
-        return self.copy(4 + n, u, 2, 3, rows, flip("mp", 1))
+        return self.copy(3 + n, u, 2, 3, self.rows(u, n == 0), flip("mp", 1))
 
     def owns(self, start, stop, begin):
         def each(u, carry):
@@ -368,44 +320,23 @@
 
         lax.fori_loop(start, stop, each, 0)
 
-    def tick(self, t):
-        def at(lag, body):
-            u = t - lag
-
-            @pl.when((u >= 0) & (u < self.pieces))
-            def _():
-                body(u)
-
-        def begin(u):
-            @pl.when(u == 0)
-            def _():
-                self.across(u).start()
-
-            @pl.when(u + 1 < self.pieces)
-            def _():
-                self.across(u + 1).start()
-
-        def got_across(u):
+    def step(self, kind, u):
+        if kind == "a":
             self.across(u).wait()
-            self.quarter(u).start()
+            if u + DEPTH < self.pieces:
+                self.across(u + DEPTH).start()
+            self.beside(u).start()
             self.pass_on(u, 0).start()
-
-        def got_quarter(u):
-            self.quarter(u).wait()
-            self.half(u).start()
+        elif kind == "b":
+            self.beside(u).wait()
             self.pass_on(u, 1).start()
-
-        def got_half(u):
-            self.half(u).wait()
-            self.pass_on(u, 2).start()
-
-        def got_all(u):
-            for n in range(3):
+        else:
+            for n in range(2):
                 self.pass_on(u, n).wait()
 
-        at(0, begin)
-        for lag, body in zip(LAGS, (got_across, got_quarter, got_half, got_all)):
-            at(lag, body)
+    def at(self, *where):
+        for kind, u in PLAN.get(where, ()):
+            self.step(kind, u)
 
 
 class Reducer:
@@ -477,7 +408,7 @@
             target[at] = value.astype(BF)
             return carry
 
-        lax.fori_loop(0, size // TILE, tile, 0)
+        lax.fori_loop(0, size // TILE, tile, 0, unroll=True)
 
     def tick(self, t):
         rest = len(self.rest)
@@ -702,7 +633,8 @@
     weights = Gather(all_w, send_g, recv_g)
     for load in loads + early[3:]:
         load.wait()
-    weights.tick(0)
+    for u in range(DEPTH):
+        weights.across(u).start()
     weights.owns(0, weights.pieces, True)
     load_cot.start()
     for n, ref in enumerate((gain1, bias1, gain2, bias2, bias_out, bias_down)):
@@ -720,48 +652,45 @@
         copy.wait()
     proj = mlp.at[: 3 * local, :wide]
 
-    def gather_step(t, carry):
-        weights.tick(t)
-        return carry
-
-    reached = [1]
-
-    def gather_to(n):
-        if PLAN[n] > reached[0]:
-            lax.fori_loop(reached[0], PLAN[n], gather_step, 0)
-            reached[0] = PLAN[n]
-
     first_rows = 3 * local // PIECE
     for r in range(parts):
-        gather_to(2 * r)
+        weights.at("p", r, 0)
         if r == 1:
             weights.owns(0, first_rows, False)
         attend_chunk(
-            r, heads, rows, normed1, all_w, functools.partial(gather_to, 2 * r + 1), small, place, feats,
+            r, heads, rows, normed1, all_w, functools.partial(weights.at, "p", r), small, place, feats,
             q_all, k_all, v_all, lse, att, cosine, sine, proj,
         )
     weights.owns(first_rows, weights.pieces, False)
     load_cot.wait()
     g[...] = (slope[...] * keep_col[...]).astype(BF)
-    gather_to(2 * parts)
-    done = reached[0]
+    weights.at("w", 0, 0)
     wo = jnp.concatenate([all_w[r, 3 * local : top] for r in range(parts)])
     normed2 = branch.at[:rows]
     second_norm(rows, tokens, vec, att, wo, middle, normed2)
     mlp[...] = jnp.zeros_like(mlp)
     gsecond[...] = jnp.zeros_like(gsecond)
 
+    net = Reducer(grads, got1, got3, got2, got_dp, send, recv)
+
+    def between(r, n):
+        for k in range(parts):
+            if ("f", k, n + 1) in PLAN:
+                pl.when(r == k)(functools.partial(weights.at, "f", k, n + 1))
+        if n > 0:
+            @pl.when(r == parts - 1)
+            def _():
+                net.tick(n - 1)
+
     def mlp_step(r, carry):
         mlp_chunk(
             r, normed2, g, all_w.at[r, up_rows], all_w.at[r, down_rows], small, mlp, gsecond,
-            grads.at[r, pl.ds(0, mlp_rows)], sums_up, active, slope, lambda n: weights.tick(done + 3 * r + n),
+            grads.at[r, pl.ds(0, mlp_rows)], sums_up, active, slope, functools.partial(between, r),
         )
         return carry
 
-    assert done + 6 >= weights.ticks
     lax.fori_loop(0, parts, mlp_step, 0)
     load_cot.start()
-    net = Reducer(grads, got1, got3, got2, got_dp, send, recv)
 
     def step(t, carry):
         net.tick(t)
@@ -770,32 +699,34 @@
     def ticks(start, stop):
         lax.fori_loop(start, stop, step, 0)
 
-    ticks(0, 1)
     load_cot.wait()
     finish_mlp(slope, keep_col, vec, middle, mlp, gsecond, g, active, branch, sums_vec)
     store_out = pltpu.make_async_copy(active, out, local_sem.at[6])
     store_out.start()
-    ticks(1, 2)
+    ticks(3, 4)
     gatt = all_w.at[0, down_rows, :wide]
     gqkv = all_w.at[:, pl.ds(top, 3 * local), :wide]
     wo = jnp.concatenate([all_w[r, 3 * local : top] for r in range(parts)])
     gatt[...] = nt(wo, branch[...]).astype(BF)
 
+    per = 2
+
     def some_heads(i, carry):
-        net.tick(2 + i)
+        net.tick(4 + i)
 
         def head(n, c):
-            attend_back(2 * i + n, heads, rows, q_all, k_all, v_all, lse, att, gatt, cosine, sine, place, gqkv, column, head_sums)
+            attend_back(per * i + n, heads, rows, q_all, k_all, v_all, lse, att, gatt, cosine, sine, place, gqkv, column, head_sums)
             return c
 
-        return lax.fori_loop(0, 2, head, carry)
-
-    lax.fori_loop(0, count // 2, some_heads, 0)
-    base = 2 + count // 2
+        return lax.fori_loop(0, per, head, carry)
+
+    lax.fori_loop(0, count // per, some_heads, 0)
+    base = 4 + count // per
+    assert count % per == 0 and base + parts // 2 <= mlp_rows // UNIT
     gsecond[...] = jnp.zeros_like(gsecond)
 
     def late(r, carry):
-        net.tick(base + r)
+        pl.when(r % 2 == 0)(lambda: net.tick(base + r // 2))
         here = att[pl.ds(pl.multiple_of(r * local, HD), local)]
         grads[r, mlp_rows : mlp_rows + local] = nn(here, branch[...]).astype(BF)
         grads[r, mlp_rows + local :] = nn(gqkv[r], normed1[...]).astype(BF)
@@ -803,7 +734,7 @@
         return carry
 
     lax.fori_loop(0, parts, late, 0)
-    base = base + parts
+    base = base + parts // 2
     ticks(base, base + 1)
     grad = gsecond[...]
     unit, scale = unit_of(tokens[...].astype(F32))
@@ -839,10 +770,11 @@
         return carry
 
     lax.fori_loop(base, base + exchanges + 1, step_small, 0)
-    ticks(base + exchanges + 1, max(net.ticks, base + exchanges + 1))
     stores = []
     start = 0
-    for n, ref in enumerate((o_up, o_down, o_out, o_qkv)):
+    for n, ref in enumerate((o_down, o_up, o_out, o_qkv)):
+        if n == 2:
+            ticks(base + exchanges + 1, max(net.ticks, base + exchanges + 1))
         stores.append(pltpu.make_async_copy(grads.at[1, pl.ds(start, ref.shape[0])], ref, local_sem.at[8 + n]))
         stores[-1].start()
         start += ref.shape[0]
@@ -851,38 +783,33 @@
 
 
 def finish_body(vectors, local, up, down, out, qkv, small, factor, middle, gx, *rest):
-    results, (held, held_gx, copies) = rest[:-3], rest[-3:]
-    loads = [pltpu.make_async_copy(middle, held, copies.at[0]), pltpu.make_async_copy(gx, held_gx, copies.at[1])]
-    moves = [pltpu.make_async_copy(held, results[-2], copies.at[2]), pltpu.make_async_copy(held_gx, results[-1], copies.at[3])]
-
-    @pl.when(pl.program_id(0) == 0)
-    def _():
-        for load in loads:
-            load.start()
-        for n, row in enumerate(vectors):
-            results[4 + n][...] = small[row : row + 1].reshape(small.shape[1])
-        b_qkv, freqs = results[4 + len(vectors)], results[5 + len(vectors)]
-        for n in range(3):
-            b_qkv[n : n + 1] = small[9:10, n * local : (n + 1) * local]
-        for n in range(2):
-            for h in range(freqs.shape[0]):
-                start = 3 * local + (n * freqs.shape[0] + h) * HALF
-                freqs[h, n : n + 1] = small[9:10, start : start + HALF]
-
-    for source, target in zip((up, down, out, qkv), results):
-        target[...] = source[...].astype(F32) * factor[0]
-
-    @pl.when(pl.program_id(0) == 2)
-    def _():
-        for load in loads:
-            load.wait()
-        for move in moves:
-            move.start()
-
-    @pl.when(pl.program_id(0) == pl.num_programs(0) - 1)
-    def _():
-        for move in moves:
-            move.wait()
+    shared = len(vectors) + 2
+    results, rest = rest[: 6 + shared], rest[6 + shared :]
+    low, full, copies = rest[:6], rest[6:10], rest[10]
+    sources = (up, down, out, qkv, middle, gx)
+    targets = results[:4] + results[4 + shared :]
+    loads = [pltpu.make_async_copy(a, b, copies.at[0, n]) for n, (a, b) in enumerate(zip(sources, low))]
+    ready = full + low[4:]
+    stores = [pltpu.make_async_copy(a, b, copies.at[1, n]) for n, (a, b) in enumerate(zip(ready, targets))]
+    order = (3, 2, 0, 1, 5, 4)
+    for n in order:
+        loads[n].start()
+    for n, row in enumerate(vectors):
+        results[4 + n][...] = small[row : row + 1].reshape(small.shape[1])
+    b_qkv, freqs = results[4 + len(vectors)], results[5 + len(vectors)]
+    for n in range(3):
+        b_qkv[n : n + 1] = small[9:10, n * local : (n + 1) * local]
+    for n in range(2):
+        for h in range(freqs.shape[0]):
+            start = 3 * local + (n * freqs.shape[0] + h) * HALF
+            freqs[h, n : n + 1] = small[9:10, start : start + HALF]
+    for n in order:
+        loads[n].wait()
+        if n < 4:
+            full[n][...] = low[n][...].astype(F32) * factor[0]
+        stores[n].start()
+    for n in order:
+        stores[n].wait()
 
 
 def sds(shape, dtype):
@@ -984,8 +911,8 @@
             vmem((SLOTS * UNIT, width), BF),
             vmem((SLOTS * UNIT, width), BF),
             vmem((swaps, 16, width), F32),
-            dma((7, pieces)),
-            dma((7, pieces)),
+            dma((5, pieces)),
+            dma((5, pieces)),
             dma((3,)),
             dma((3,)),
             dma((24,)),
@@ -999,22 +926,19 @@
         compiler_params=pltpu.CompilerParams(vmem_limit_bytes=61 << 20, collective_id=0, has_side_effects=True),
     )(tokens, norm1_gain, norm1_bias, norm2_gain, norm2_bias, b_out, b_down, positions, keep_mask, b_qkv,
       rotary_freqs.transpose(1, 0, 2), b_up, image_group, cotangent, w_qkv_t, w_out, w_up, w_down)
-    steps = 6
-
-    def piece(ref):
-        return pl.BlockSpec((ref.shape[0] // steps, width), lambda i: (i, 0))
-
     sums = (o_up, o_down, o_out, o_qkv)
     vectors = [0, 1, 2, 3, 4, 5, 8]
     finished = pl.pallas_call(
         functools.partial(finish_body, vectors, local),
-        grid=(steps,),
         out_shape=[sds(ref.shape, F32) for ref in sums]
         + [sds((width,), F32)] * len(vectors)
         + [sds((3, local), F32), sds((heads, 2, HALF), F32), sds(out.shape, BF), sds(gx.shape, F32)],
-        in_specs=[piece(ref) for ref in sums] + [in_vmem, in_smem, anywhere, anywhere],
-        out_specs=[piece(ref) for ref in sums] + [in_vmem] * (len(vectors) + 2) + [anywhere] * 2,
-        scratch_shapes=[vmem(out.shape, BF), vmem(gx.shape, F32), dma((4,))],
+        in_specs=[anywhere] * 4 + [in_vmem, in_smem, anywhere, anywhere],
+        out_specs=[anywhere] * 4 + [in_vmem] * (len(vectors) + 2) + [anywhere] * 2,
+        scratch_shapes=[vmem(ref.shape, BF) for ref in sums]
+        + [vmem(out.shape, BF), vmem(gx.shape, F32)]
+        + [vmem(ref.shape, F32) for ref in sums]
+        + [dma((2, 6))],
         compiler_params=pltpu.CompilerParams(vmem_limit_bytes=60 << 20),
     )(*sums, small_sum, factor, out, gx)
     sum_w_up, sum_w_down, sum_w_out, sum_w_qkv, gain1, bias1, b_out_sum, gain2, bias2, b_down_sum, b_up_sum = finished[:11]

time: 189 us -> 181 us (0.958)
  Pallas kernels: 188 us -> 179 us
    pallas_call x1, Pallas kernels: 179 us -> 172 us  [body(): pl.pallas_call(functools.partial(layer_body, heads, rows), out_shape=[sds...]
    pallas_call x1, Pallas kernels: 9.21 us -> 7.19 us  [body(): pl.pallas_call(functools.partial(finish_body, vectors, local), out_shape=...]
where the time goes in v1:
time: 181 us
  Pallas kernels  179 us (99%)
    pallas_call x1, Pallas kernels, body(): pl.pallas_call(functools.partial(layer_body, heads, rows), out_shape=[sds...  172 us
    pallas_call x1, Pallas kernels, body(): pl.pallas_call(functools.partial(finish_body, vectors, local), out_shape=...  7.19 us

profile of v1, /device:TPU:0, one launch (start us, length us, event | category | flops | bytes accessed | tf_op | source)
XLA Modules:
  0.0 180.9 jit_solution(1995993238330711181)
XLA Ops:
  1.3 172.2 %shard_map.289 = (bf16[592,768]{1,0:T(8,128)(2,1)}, f32[592,768]{1,0:T(8,128)}, bf16[768,768]{1,0:T(8,128)(2,1)}, bf16[768,768]{1,0:T(8,128)(2,1)}, bf16[192,768...) custom-call(bf16[592,768]{1,0:T(8,128)(2,1)} %tokens_in.1, f32[768]{0:T(1024)} %gain1_in.1, ...), custom_call_target="tpu_custom_call" | custom-call | tf_op jit(solution)/shard_map/pallas_call | solution.py:860
  173.5 7.2 %shard_map.290 = (f32[768,768]{1,0:T(8,128)}, f32[768,768]{1,0:T(8,128)}, f32[192,768]{1,0:T(8,128)}, f32[576,768]{1,0:T(8,128)}, f32[768]{0:T(1024)}, /*index=5...) custom-call(bf16[768,768]{1,0:T(8,128)(2,1)} %get-tuple-element.38.u, ...), custom_call_target="tpu_custom_call" | custom-call | tf_op jit(solution)/shard_map/pallas_call | solution.py:931

commit v2 on v1

--- a/solution.py
+++ b/solution.py
@@ -84,14 +84,19 @@
     keep[...] = place[...].T[:rows, 2:3]
 
 
+def turns(r, heads, small, place, cosine, sine):
+    start = 3 * heads * HD
+    column = small[r].T[:, 1:2]
+    f0 = column[start : start + heads * HALF]
+    f1 = column[start + heads * HALF : start + 2 * heads * HALF]
+    angles = f0 * place[0:1] + f1 * place[1:2]
+    cosine[r] = jnp.cos(angles)
+    sine[r] = jnp.sin(angles)
+
+
 def attend_chunk(r, heads, rows, normed1, weights, hook, small, place, feats, q_all, k_all, v_all, lse, att, cosine, sine, proj):
     local = heads * HD
     column = small[r].T[:, 1:2]
-    f0 = column[3 * local : 3 * local + heads * HALF]
-    f1 = column[3 * local + heads * HALF : 3 * local + 2 * heads * HALF]
-    angles = f0 * place[0:1] + f1 * place[1:2]
-    cosine[r] = jnp.cos(angles)
-    sine[r] = jnp.sin(angles)
     proj[...] = nt(weights[r, : 3 * local], normed1[...]) + column[: 3 * local]
     hook(1)
     for h in range(heads):
@@ -211,29 +216,31 @@
 UNIT = 128
 PIECE = 192
 DEPTH = 3
+SIZES = (192, 192, 192, 192, 192, 192, 192, 192, 192, 192, 192, 192)
 PLAN = {
     ('p', 0, 2): (('a', 0),),
     ('p', 1, 1): (('a', 1),),
     ('p', 1, 3): (('a', 2), ('b', 0)),
-    ('p', 2, 0): (('d', 0), ('a', 3), ('b', 1), ('d', 1), ('a', 4), ('b', 2)),
+    ('p', 4, 0): (('d', 0),),
+    ('p', 4, 1): (('a', 3),),
+    ('p', 2, 0): (('b', 1), ('d', 1), ('a', 4), ('b', 2)),
     ('p', 2, 1): (('d', 2),),
-    ('p', 2, 2): (('b', 3), ('a', 5)),
-    ('p', 2, 3): (('d', 3),),
-    ('p', 3, 1): (('b', 4), ('a', 6)),
-    ('p', 3, 2): (('d', 4),),
-    ('p', 3, 3): (('a', 7), ('b', 5)),
-    ('w', 0, 0): (('d', 5),),
-    ('f', 0, 0): (('a', 8), ('b', 6)),
-    ('f', 0, 1): (('d', 6), ('a', 9), ('b', 7)),
-    ('f', 0, 2): (('d', 7),),
-    ('f', 0, 3): (('a', 10),),
-    ('f', 0, 4): (('b', 8),),
-    ('f', 1, 0): (('d', 8), ('a', 11)),
-    ('f', 1, 1): (('b', 9),),
-    ('f', 1, 2): (('d', 9),),
-    ('f', 1, 3): (('b', 10),),
-    ('f', 1, 4): (('d', 10), ('b', 11)),
-    ('f', 2, 0): (('d', 11),),
+    ('p', 2, 3): (('b', 3), ('a', 5)),
+    ('p', 3, 0): (('d', 3),),
+    ('p', 3, 2): (('b', 4), ('a', 6)),
+    ('p', 3, 3): (('d', 4),),
+    ('f', 0, 0): (('a', 7), ('b', 5)),
+    ('f', 0, 1): (('a', 8), ('d', 5), ('b', 6)),
+    ('f', 0, 2): (('d', 6),),
+    ('f', 0, 3): (('a', 9),),
+    ('f', 0, 4): (('b', 7),),
+    ('f', 1, 0): (('a', 10), ('d', 7)),
+    ('f', 1, 1): (('b', 8),),
+    ('f', 1, 2): (('a', 11), ('d', 8)),
+    ('f', 1, 3): (('b', 9),),
+    ('f', 1, 4): (('b', 10), ('d', 9)),
+    ('f', 2, 0): (('d', 10), ('b', 11)),
+    ('f', 2, 1): (('d', 11),),
 }
 SLOTS = 6
 TILE = 16
@@ -282,12 +289,13 @@
 class Gather:
     def __init__(self, weights, send, recv):
         self.weights, self.send, self.recv = weights, send, recv
-        self.pieces = weights.shape[1] // PIECE
+        self.pieces = len(SIZES)
+        assert sum(SIZES) == weights.shape[1]
 
     def rows(self, u, mine):
-        half = PIECE // 2
+        start, half = sum(SIZES[:u]), SIZES[u] // 2
         upper = bit_of("dp", 1 + u % 2)
-        return pl.ds(pl.multiple_of(u * PIECE + (upper if mine else 1 - upper) * half, TILE), half)
+        return pl.ds(pl.multiple_of(start + (upper if mine else 1 - upper) * half, TILE), half)
 
     def copy(self, stage, u, source, target, rows, peer):
         return remote(
@@ -635,7 +643,8 @@
         load.wait()
     for u in range(DEPTH):
         weights.across(u).start()
-    weights.owns(0, weights.pieces, True)
+    own_pieces = all_w.shape[1] // PIECE
+    weights.owns(0, own_pieces, True)
     load_cot.start()
     for n, ref in enumerate((gain1, bias1, gain2, bias2, bias_out, bias_down)):
         vec[n : n + 1] = ref[...].reshape(1, width)
@@ -654,6 +663,15 @@
 
     first_rows = 3 * local // PIECE
     for r in range(parts):
+        if r < 2:
+            turns(r, heads, small, place, cosine, sine)
+        if r == 2:
+            for n in range(2):
+                weights.at("p", parts, n)
+                turns(r + n, heads, small, place, cosine, sine)
+            load_cot.wait()
+            g[...] = (slope[...] * keep_col[...]).astype(BF)
+            gsecond[...] = jnp.zeros_like(gsecond)
         weights.at("p", r, 0)
         if r == 1:
             weights.owns(0, first_rows, False)
@@ -661,15 +679,12 @@
             r, heads, rows, normed1, all_w, functools.partial(weights.at, "p", r), small, place, feats,
             q_all, k_all, v_all, lse, att, cosine, sine, proj,
         )
-    weights.owns(first_rows, weights.pieces, False)
-    load_cot.wait()
-    g[...] = (slope[...] * keep_col[...]).astype(BF)
+    weights.owns(first_rows, own_pieces, False)
     weights.at("w", 0, 0)
     wo = jnp.concatenate([all_w[r, 3 * local : top] for r in range(parts)])
     normed2 = branch.at[:rows]
     second_norm(rows, tokens, vec, att, wo, middle, normed2)
     mlp[...] = jnp.zeros_like(mlp)
-    gsecond[...] = jnp.zeros_like(gsecond)
 
     net = Reducer(grads, got1, got3, got2, got_dp, send, recv)
 
@@ -850,7 +865,7 @@
     stages = 8 + len(bits)
     total_rows = 2 * width + 4 * local
     unit_count = total_rows // UNIT
-    pieces = total_rows // PIECE
+    pieces = max(total_rows // PIECE, len(SIZES))
     swaps = 2 + len(bits)
     in_vmem = pl.BlockSpec(memory_space=pltpu.VMEM)
     in_smem = pl.BlockSpec(memory_space=pltpu.SMEM)

time: 181 us -> 177 us (0.978)
  Pallas kernels: 179 us -> 176 us
    pallas_call x1, Pallas kernels: 172 us -> 169 us  [body(): pl.pallas_call(functools.partial(layer_body, heads, rows), out_shape=[sds...]
where the time goes in v2:
time: 177 us
  Pallas kernels  176 us (99%)
    pallas_call x1, Pallas kernels, body(): pl.pallas_call(functools.partial(layer_body, heads, rows), out_shape=[sds...  169 us
    pallas_call x1, Pallas kernels, body(): pl.pallas_call(functools.partial(finish_body, vectors, local), out_shape=...  7.19 us

profile of v2, /device:TPU:0, one launch (start us, length us, event | category | flops | bytes accessed | tf_op | source)
XLA Modules:
  0.0 177.2 jit_solution(12800462755126257496)
XLA Ops:
  1.3 168.5 %shard_map.289 = (bf16[592,768]{1,0:T(8,128)(2,1)}, f32[592,768]{1,0:T(8,128)}, bf16[768,768]{1,0:T(8,128)(2,1)}, bf16[768,768]{1,0:T(8,128)(2,1)}, bf16[192,768...) custom-call(bf16[592,768]{1,0:T(8,128)(2,1)} %tokens_in.1, f32[768]{0:T(1024)} %gain1_in.1, ...), custom_call_target="tpu_custom_call" | custom-call | tf_op jit(solution)/shard_map/pallas_call | solution.py:875
  169.8 7.2 %shard_map.290 = (f32[768,768]{1,0:T(8,128)}, f32[768,768]{1,0:T(8,128)}, f32[192,768]{1,0:T(8,128)}, f32[576,768]{1,0:T(8,128)}, f32[768]{0:T(1024)}, /*index=5...) custom-call(bf16[768,768]{1,0:T(8,128)(2,1)} %get-tuple-element.38.u, ...), custom_call_target="tpu_custom_call" | custom-call | tf_op jit(solution)/shard_map/pallas_call | solution.py:946

commit v3 on v2

--- a/solution.py
+++ b/solution.py
@@ -745,12 +745,19 @@
         here = att[pl.ds(pl.multiple_of(r * local, HD), local)]
         grads[r, mlp_rows : mlp_rows + local] = nn(here, branch[...]).astype(BF)
         grads[r, mlp_rows + local :] = nn(gqkv[r], normed1[...]).astype(BF)
+        return carry
+
+    lax.fori_loop(0, parts, late, 0)
+    base = base + parts // 2
+
+    def back(r, carry):
+        pl.when(r % 2 == 0)(lambda: net.tick(base + r // 2))
         gsecond[...] += tn(gqkv[r], all_w[r, : 3 * local])[:rows]
         return carry
 
-    lax.fori_loop(0, parts, late, 0)
-    base = base + parts // 2
-    ticks(base, base + 1)
+    lax.fori_loop(0, parts, back, 0)
+    late_done = base + parts // 2
+    ticks(late_done, late_done + 1)
     grad = gsecond[...]
     unit, scale = unit_of(tokens[...].astype(F32))
     gsecond[...] = middle[...] + norm_back(grad, unit, scale, vec[0:1])
@@ -766,7 +773,7 @@
         pieces = [v[:, n * HD : (n + 1) * HD] for n in range(3) for v in mine]
         pieces += [v[:, 3 * HD + n * HALF : 3 * HD + (n + 1) * HALF] for n in range(2) for v in mine]
         small_sum[9 + 2 * r : 10 + 2 * r] = jnp.concatenate(pieces, axis=1)
-    base = base + 1
+    base = late_done + 1
     exchanges = len(sums.peers)
 
     def step_small(t, carry):

time: 177 us -> 179 us (1.011)
  no operation moved by 1% of the time
where the time goes in v3:
time: 179 us
  Pallas kernels  177 us (99%)
    pallas_call x1, Pallas kernels, body(): pl.pallas_call(functools.partial(layer_body, heads, rows), out_shape=[sds...  170 us
    pallas_call x1, Pallas kernels, body(): pl.pallas_call(functools.partial(finish_body, vectors, local), out_shape=...  7.19 us

profile of v3, /device:TPU:0, one launch (start us, length us, event | category | flops | bytes accessed | tf_op | source)
XLA Modules:
  0.0 178.6 jit_solution(10193504996804198250)
XLA Ops:
  1.3 170.0 %shard_map.289 = (bf16[592,768]{1,0:T(8,128)(2,1)}, f32[592,768]{1,0:T(8,128)}, bf16[768,768]{1,0:T(8,128)(2,1)}, bf16[768,768]{1,0:T(8,128)(2,1)}, bf16[192,768...) custom-call(bf16[592,768]{1,0:T(8,128)(2,1)} %tokens_in.1, f32[768]{0:T(1024)} %gain1_in.1, ...), custom_call_target="tpu_custom_call" | custom-call | tf_op jit(solution)/shard_map/pallas_call | solution.py:882
  171.3 7.2 %shard_map.290 = (f32[768,768]{1,0:T(8,128)}, f32[768,768]{1,0:T(8,128)}, f32[192,768]{1,0:T(8,128)}, f32[576,768]{1,0:T(8,128)}, f32[768]{0:T(1024)}, /*index=5...) custom-call(bf16[768,768]{1,0:T(8,128)(2,1)} %get-tuple-element.38.u, ...), custom_call_target="tpu_custom_call" | custom-call | tf_op jit(solution)/shard_map/pallas_call | solution.py:953
